TPU v7x, 32 devices: a whole 2x2x4 slice. The times are simulated.
32 devices in a mesh: groups: 2 (over y), head: 8 (over z, x), blk: 2 (over core).
Axes of the slice: x: 2, y: 2, z: 4, core: 2. Of those that a mesh axis runs over, the one named last changes fastest.
Arguments:
- queries: bfloat16 [256, 4096], P(('groups', 'head', 'blk')), parts along dimension 0, may hold values from -36 to 36
- keys: bfloat16 [256, 4096], P(('groups', 'head', 'blk')), parts along dimension 0, may hold values from -6 to 6
- values: bfloat16 [256, 4096], P(('groups', 'head', 'blk')), parts along dimension 0, may hold values from -12 to 12
- tile_mask: int32 [64, 1, 1], P('groups'), parts along dimension 0, may hold values from 0 to 1, as said below
Outputs:
- attended: bfloat16 [256, 4096], P(('groups', 'head', 'blk')), parts along dimension 0
There are 2 independent parts, one for each index of `groups`. A program takes and returns all parts, laid end to end along the dimension named above; each array names one. Nothing has to cross between parts.
Inputs may be any that keep to these rules, and one draw needn't show every extreme that they name: tile_mask[h, t, t] = 1 for every head h and query tile t.
All inputs are finite; a program needn't handle non-finite values.
Results may differ from a plain program's by a relative error of at most 0.005.
Values may be sent and summed in bfloat16 or wider, within the bound.
No kernel may reach another device: no remote copies, remote signals or barrier semaphores. Data moves between devices by JAX's collectives and lax.ppermute only.
A program may use at most 64 MiB of HBM per device.

v0:
```python
import jax
import jax.numpy as jnp
from jax import lax
from jax.sharding import PartitionSpec as P

H = 32
HD = 128
TILE = 128
big_negative = -1e30


def from_behind(array, axis, by):
    count = lax.axis_size(axis)
    return lax.ppermute(array, axis, [(i, (i + by) % count) for i in range(count)])


def update_block(inputs, k_rows, v_rows, k_tiles, heads_mask, score_scale):
    q_piece, q_tiles, out_sum, row_top, row_total = inputs
    rows_mask = jnp.take(heads_mask, q_tiles, axis=1)
    allowed = jnp.take(rows_mask, k_tiles, axis=2) > 0
    scores = (
        jnp.einsum("qhd,khd->hqk", q_piece, k_rows, preferred_element_type=jnp.float32)
        * score_scale
    )
    scores = jnp.where(allowed, scores, big_negative)
    new_top = jnp.maximum(row_top, jnp.max(scores, axis=2))
    factor = jnp.exp(row_top - new_top)
    weights = jnp.where(allowed, jnp.exp(scores - new_top[:, :, None]), 0.0)
    row_total = row_total * factor + jnp.sum(weights, axis=2)
    out_sum = out_sum * factor[:, :, None] + jnp.einsum(
        "hqk,khd->hqd", weights.astype(jnp.bfloat16), v_rows, preferred_element_type=jnp.float32
    )
    return (out_sum, new_top, row_total)


def attend(q_in, q_index, stacked, key_index_of, pass_on, heads_mask, per_dev, blk_count, my_blk):
    q_rows = q_in.reshape(-1, per_dev, HD)
    row_count = q_rows.shape[0]
    block_count = row_count // row_count
    q_blocks = q_rows.reshape(block_count, row_count, per_dev, HD)
    q_tiles = (q_index // TILE).reshape(block_count, row_count)
    out_sum = jnp.zeros((block_count, per_dev, row_count, HD), jnp.float32)
    row_top = jnp.full((block_count, per_dev, row_count), big_negative, jnp.float32)
    row_total = jnp.zeros((block_count, per_dev, row_count), jnp.float32)
    kv_pair = stacked
    for cycle_step in range(blk_count):
        if cycle_step > 0:
            kv_pair = pass_on(kv_pair)
        k_tiles = key_index_of((my_blk - cycle_step) % blk_count) // TILE
        k_rows = kv_pair[0].reshape(-1, per_dev, HD)
        v_rows = kv_pair[1].reshape(-1, per_dev, HD)

        def step_block(inputs):
            return update_block(inputs, k_rows, v_rows, k_tiles, heads_mask, HD ** (-0.5))

        out_sum, row_top, row_total = lax.map(
            step_block, (q_blocks, q_tiles, out_sum, row_top, row_total)
        )
    out_sum = out_sum.transpose(0, 2, 1, 3).reshape(row_count, per_dev, HD)
    row_top = row_top.transpose(0, 2, 1).reshape(row_count, per_dev)
    row_total = row_total.transpose(0, 2, 1).reshape(row_count, per_dev)
    return (out_sum, row_top, row_total)


def on_device(queries, keys, values, tile_mask):
    head_count = lax.axis_size("head")
    blk_count = lax.axis_size("blk")
    my_head = lax.axis_index("head")
    my_blk = lax.axis_index("blk")
    per_dev = max(1, H // head_count)
    split_count = max(1, head_count // H)
    groups = head_count // split_count
    row_width = per_dev * HD
    query_count = queries.shape[0]
    key_count = keys.shape[0]
    part_id = my_head % split_count
    heads_mask = lax.dynamic_slice_in_dim(tile_mask, my_head // split_count * per_dev, per_dev, 0)
    source = jnp.arange(head_count, dtype=jnp.int32)

    def copy_rows(matrix, row_count):
        shaped = matrix.reshape(row_count, groups, row_width).transpose(1, 0, 2)[:, None]
        return jnp.broadcast_to(shaped, (groups, split_count, row_count, row_width)).reshape(
            head_count, row_count, row_width
        )

    def index_of(per_source, offset, row_count, src_blk):
        starts = (source[:, None] * blk_count + src_blk) * per_source + offset
        return (starts + jnp.arange(row_count, dtype=jnp.int32)[None, :]).reshape(-1)

    sub_rows = query_count // split_count
    shaped = queries.reshape(split_count, query_count // split_count, groups, row_width)
    q_in = lax.all_to_all(
        shaped.transpose(2, 0, 1, 3).reshape(head_count, query_count // split_count, row_width),
        "head",
        split_axis=0,
        concat_axis=0,
        tiled=True,
    )
    k_in, v_in = (
        lax.all_to_all(copy_rows(keys, key_count), "head", split_axis=0, concat_axis=0, tiled=True),
        lax.all_to_all(
            copy_rows(values, key_count), "head", split_axis=0, concat_axis=0, tiled=True
        ),
    )
    kv_stack = jnp.stack([k_in, v_in])

    def pass_on(kv_pair):
        return from_behind(kv_pair, "blk", 1)

    def key_index_of(src_blk):
        return index_of(key_count, 0, key_count, src_blk)

    q_index = index_of(query_count, part_id * sub_rows, sub_rows, my_blk)
    out_sum, row_top, row_total = attend(
        q_in, q_index, kv_stack, key_index_of, pass_on, heads_mask, per_dev, blk_count, my_blk
    )
    result = (
        (out_sum / row_total[:, :, None])
        .astype(jnp.bfloat16)
        .reshape(head_count, sub_rows, row_width)
    )
    returned = lax.all_to_all(result, "head", split_axis=0, concat_axis=0, tiled=True)
    attended = (
        returned.reshape(groups, split_count, sub_rows, row_width)
        .transpose(1, 2, 0, 3)
        .reshape(query_count, H * HD)
    )
    return attended


def solution(mesh):
    in_specs = (
        P(("groups", "head", "blk"), None),
        P(("groups", "head", "blk"), None),
        P(("groups", "head", "blk"), None),
        P("groups", None, None),
    )
    out_specs = P(("groups", "head", "blk"), None)
    return jax.shard_map(
        on_device, mesh=mesh, in_specs=in_specs, out_specs=out_specs, check_vma=False
    )
```

profile of v0, /device:TPU:0, one launch (start us, length us, event | category | flops | bytes accessed | tf_op | source)
XLA Modules:
  0.0 46.3 jit_solution(11785490552753711157)
XLA Ops:
  0.0 7.4 %all-to-all-start.1 = ((bf16[8,8,512]{2,1,0:T(8,128)(2,1)}), bf16[8,8,512]{2,1,0:T(8,128)(2,1)S(1)}, u32[]{:S(2)}, u32[]{:S(2)}) async-start(bf16[8,8,512]{2,1,0:T(8,128)(2,1)} %bitcast.59), calls=%async_computation.1 | async-start | bytes 131072 | tf_op jit(solution)/shard_map/all_to_all | solution.py:100
  7.4 0.1 iota_add_fusion.2
  7.5 0.1 add.154
  7.7 0.1 add.161
  7.8 0.1 iota_add_fusion
  7.9 0.1 add.169
  8.0 0.1 dynamic-slice_bitcast_fusion
  8.0 0.1 select_bitcast_fusion
  8.1 6.2 %all-to-all-done.1 = bf16[8,8,512]{2,1,0:T(8,128)(2,1)S(1)} async-done(((bf16[8,8,512]{2,1,0:T(8,128)(2,1)}), bf16[8,8,512]{2,1,0:T(8,128)(2,1)S(1)}, u32[]{:S(2)}, u32[]{:S(2)}) %all-to-all-start.1) | async-done | bytes 65568 | tf_op jit(solution)/shard_map/all_to_all | solution.py:100
  14.3 3.4 %all-to-all-start.2 = ((bf16[8,8,512]{2,1,0:T(8,128)(2,1)}), bf16[8,8,512]{2,1,0:T(8,128)(2,1)S(1)}, u32[]{:S(2)}, u32[]{:S(2)}) async-start(bf16[8,8,512]{2,1,0:T(8,128)(2,1)} %bitcast.8), calls=%async_computation.2 | async-start | bytes 131072 | tf_op jit(solution)/shard_map/all_to_all | solution.py:101
  17.7 6.8 %all-to-all-done.2 = bf16[8,8,512]{2,1,0:T(8,128)(2,1)S(1)} async-done(((bf16[8,8,512]{2,1,0:T(8,128)(2,1)}), bf16[8,8,512]{2,1,0:T(8,128)(2,1)S(1)}, u32[]{:S(2)}, u32[]{:S(2)}) %all-to-all-start.2) | async-done | bytes 65568 | tf_op jit(solution)/shard_map/all_to_all | solution.py:101
  24.5 3.4 %all-to-all-start = ((bf16[8,8,512]{2,1,0:T(8,128)(2,1)}), bf16[8,8,512]{2,1,0:T(8,128)(2,1)S(1)}, u32[]{:S(2)}, u32[]{:S(2)}) async-start(bf16[8,8,512]{2,1,0:T(8,128)(2,1)} %bitcast.4), calls=%async_computation | async-start | bytes 131072 | tf_op jit(solution)/shard_map/all_to_all | solution.py:92
  27.9 0.1 collective-permute-start
  28.0 6.7 %all-to-all-done = bf16[8,8,512]{2,1,0:T(8,128)(2,1)S(1)} async-done(((bf16[8,8,512]{2,1,0:T(8,128)(2,1)}), bf16[8,8,512]{2,1,0:T(8,128)(2,1)S(1)}, u32[]{:S(2)}, u32[]{:S(2)}) %all-to-all-start) | async-done | bytes 65568 | tf_op jit(solution)/shard_map/all_to_all | solution.py:92
  34.7 0.2 fusion.46
  35.0 0.2 fusion.45
  35.2 0.1 fusion.7
  35.4 0.3 fusion.3
  35.6 0.3 fusion
  35.9 0.1 copy.18
  36.1 0.1 copy.19
  36.2 0.1 div.54
  36.4 9.3 %all_to_all.20 = bf16[8,8,512]{2,1,0:T(8,128)(2,1)S(1)} all-to-all(bf16[8,8,512]{2,1,0:T(8,128)(2,1)S(1)} %divide_convert_fusion), channel_id=1, replica_groups=mesh['groups'=2,'head'=8,'blk'=2] {'head'}, dimensions={0} | all-to-all | bytes 131072 | tf_op jit(solution)/shard_map/all_to_all | solution.py:122
  45.7 0.6 %copy.43 = bf16[8,4096]{1,0:T(8,128)(2,1)} copy(bf16[8,4096]{1,0:T(8,128)(2,1)S(1)} %bitcast.58) | data formatting | bytes 131072
  (22 shorter events, 0.4 us)
Async XLA Ops:
  0.0 8.0 %copy-start = (s32[32,1,1]{0,2,1:T(1,128)S(1)}, s32[32,1,1]{0,2,1:T(1,128)}, u32[]{:S(2)}) copy-start(s32[32,1,1]{0,2,1:T(1,128)} %param.11) | copy-start | bytes 388
  0.0 14.3 %all-to-all-start.1 = ((bf16[8,8,512]{2,1,0:T(8,128)(2,1)}), bf16[8,8,512]{2,1,0:T(8,128)(2,1)S(1)}, u32[]{:S(2)}, u32[]{:S(2)}) async-start(bf16[8,8,512]{2,1,0:T(8,128)(2,1)} %bitcast.59), calls=%async_computation.1 | async-start | bytes 131072 | tf_op jit(solution)/shard_map/all_to_all | solution.py:100
  14.3 10.2 %all-to-all-start.2 = ((bf16[8,8,512]{2,1,0:T(8,128)(2,1)}), bf16[8,8,512]{2,1,0:T(8,128)(2,1)S(1)}, u32[]{:S(2)}, u32[]{:S(2)}) async-start(bf16[8,8,512]{2,1,0:T(8,128)(2,1)} %bitcast.8), calls=%async_computation.2 | async-start | bytes 131072 | tf_op jit(solution)/shard_map/all_to_all | solution.py:101
  24.5 10.2 %all-to-all-start = ((bf16[8,8,512]{2,1,0:T(8,128)(2,1)}), bf16[8,8,512]{2,1,0:T(8,128)(2,1)S(1)}, u32[]{:S(2)}, u32[]{:S(2)}) async-start(bf16[8,8,512]{2,1,0:T(8,128)(2,1)} %bitcast.4), calls=%async_computation | async-start | bytes 131072 | tf_op jit(solution)/shard_map/all_to_all | solution.py:92
  27.9 7.0 %collective-permute-start = (bf16[2,8,8,512]{3,2,1,0:T(8,128)(2,1)S(1)}, bf16[2,8,8,512]{3,2,1,0:T(8,128)(2,1)S(1)}, u32[]{:S(2)}, u32[]{:S(2)}) collective-permute-start(bf16[2,8,8,512]{3,2,1,0:T(8,128)(2,1)S(1)} %pad_maximum_fusion), channel_id=1, source_target_pairs={{0,1},{1,0},{2,3},{3,2},{4,5},{5,4},{6,7},{7,6},{8,9},{9,8},{10,11... | collective-permute-start | bytes 393224 | tf_op jit(solution)/shard_map/ppermute | solution.py:14
where the time goes:
time: 46.8 us; the launch traced here: 46.3 us
  waiting for transfers between devices  19.7 us (42%)
  starting transfers between devices  14.2 us (30%)
  blocking collectives  9.29 us (20%)
  local copies, waits for them, and re-layouts  1.49 us (3%)
  matrix products  0.94 us (2%)
  other arithmetic  0.55 us (1%)
    all_to_all x1, blocking collectives, on_device(): lax.all_to_all(result, 'head', split_axis=0, concat_axis=0, tiled=True)  9.29 us
    all_to_all x1, starting transfers between devices, on_device(): lax.all_to_all(copy_rows(keys, key_count), 'head', split_axis=0, concat_a...  7.41 us
    all_to_all x1, waiting for transfers between devices, on_device(): lax.all_to_all(copy_rows(values, key_count), 'head', split_axis=0, concat...  6.82 us
    all_to_all x1, waiting for transfers between devices, on_device(): lax.all_to_all(shaped.transpose(2, 0, 1, 3).reshape(head_count, query_cou...  6.69 us
    all_to_all x1, waiting for transfers between devices, on_device(): lax.all_to_all(copy_rows(keys, key_count), 'head', split_axis=0, concat_a...  6.19 us
    all_to_all x1, starting transfers between devices, on_device(): lax.all_to_all(copy_rows(values, key_count), 'head', split_axis=0, concat...  3.35 us
    all_to_all x1, starting transfers between devices, on_device(): lax.all_to_all(shaped.transpose(2, 0, 1, 3).reshape(head_count, query_cou...  3.35 us
  transfers between devices with their start and end apart: 4, of which 3 were waited for; matrix products, arithmetic and copies ran while one was open for 2% of the time, Pallas kernels for 0%

commit v1 on v0

--- a/solution.py
+++ b/solution.py
@@ -7,6 +7,28 @@
 HD = 128
 TILE = 128
 big_negative = -1e30
+
+
+def in_blocks(x, dim, length):
+    before, after = (x.shape[:dim], x.shape[dim + 1 :])
+    return jnp.moveaxis(x.reshape(*before, length, -1, *after), dim, 0)
+
+
+def joined_along(blocks, dim):
+    blocks = jnp.moveaxis(blocks, 0, dim)
+    lengths = blocks.shape
+    return blocks.reshape(*lengths[:dim], lengths[dim] * lengths[dim + 1], *lengths[dim + 2 :])
+
+
+def pairwise_exchange(value, axis, split_dim, concat_dim):
+    size, here = (lax.axis_size(axis), lax.axis_index(axis))
+    pieces = in_blocks(value, split_dim, size)
+    finished = [pieces[here]]
+    for step in range(1, size):
+        sent = pieces[here ^ step]
+        finished.append(lax.ppermute(sent, axis, [(i, i ^ step) for i in range(size)]))
+    pieces = jnp.stack(finished)[here ^ jnp.arange(size)]
+    return joined_along(pieces, concat_dim)
 
 
 def from_behind(array, axis, by):
@@ -119,7 +141,7 @@
         .astype(jnp.bfloat16)
         .reshape(head_count, sub_rows, row_width)
     )
-    returned = lax.all_to_all(result, "head", split_axis=0, concat_axis=0, tiled=True)
+    returned = pairwise_exchange(result, "head", 0, 0)
     attended = (
         returned.reshape(groups, split_count, sub_rows, row_width)
         .transpose(1, 2, 0, 3)

time: 46.8 us -> 52.1 us (1.11)
  starting transfers between devices: 14.2 us -> 25.6 us
  blocking collectives: 9.29 us -> 0 us
  waiting for transfers between devices: 19.7 us -> 22 us
  local copies, waits for them, and re-layouts: 1.49 us -> 2.26 us
    ppermute x0 -> x7, starting transfers between devices: none -> 11.4 us  [pairwise_exchange(): lax.ppermute(sent, axis, [(i, i ^ step) for i in range(size)])]
    all_to_all x1 -> x0, blocking collectives: 9.29 us -> none  [on_device(): lax.all_to_all(result, 'head', split_axis=0, concat_axis=0, tiled=True)]
    ppermute x0 -> x7, waiting for transfers between devices: none -> 2.28 us  [pairwise_exchange(): lax.ppermute(sent, axis, [(i, i ^ step) for i in range(size)])]
    gather x0 -> x1, local copies, waits for them, and re-layouts: none -> 1.18 us  [pairwise_exchange(): pieces = jnp.stack(finished)[here ^ jnp.arange(size)]]
  transfers between devices with their start and end apart: 4 -> 11, of which waited for: 3 -> 5; matrix products, arithmetic and copies ran while one was open for 2% -> 2% of each run, Pallas kernels for 0% -> 0%
where the time goes in v1:
time: 52.1 us; the launch traced here: 51.7 us
  starting transfers between devices  25.6 us (49%)
  waiting for transfers between devices  22 us (42%)
  local copies, waits for them, and re-layouts  2.26 us (4%)
  matrix products  0.94 us (2%)
  other arithmetic  0.66 us (1%)
    ppermute x7, starting transfers between devices, pairwise_exchange(): lax.ppermute(sent, axis, [(i, i ^ step) for i in range(size)])  11.4 us
    all_to_all x1, starting transfers between devices, on_device(): lax.all_to_all(copy_rows(keys, key_count), 'head', split_axis=0, concat_a...  7.41 us
    all_to_all x1, waiting for transfers between devices, on_device(): lax.all_to_all(copy_rows(values, key_count), 'head', split_axis=0, concat...  6.77 us
    all_to_all x1, waiting for transfers between devices, on_device(): lax.all_to_all(shaped.transpose(2, 0, 1, 3).reshape(head_count, query_cou...  6.69 us
    all_to_all x1, waiting for transfers between devices, on_device(): lax.all_to_all(copy_rows(keys, key_count), 'head', split_axis=0, concat_a...  6.21 us
    all_to_all x1, starting transfers between devices, on_device(): lax.all_to_all(copy_rows(values, key_count), 'head', split_axis=0, concat...  3.35 us
    all_to_all x1, starting transfers between devices, on_device(): lax.all_to_all(shaped.transpose(2, 0, 1, 3).reshape(head_count, query_cou...  3.35 us
    ppermute x7, waiting for transfers between devices, pairwise_exchange(): lax.ppermute(sent, axis, [(i, i ^ step) for i in range(size)])  2.28 us
  transfers between devices with their start and end apart: 11, of which 5 were waited for; matrix products, arithmetic and copies ran while one was open for 2% of the time, Pallas kernels for 0%

profile of v1, /device:TPU:0, one launch (start us, length us, event | category | flops | bytes accessed | tf_op | source)
XLA Modules:
  0.0 51.7 jit_solution(6219381288531490787)
XLA Ops:
  0.0 7.4 %all-to-all-start.1 = ((bf16[8,8,512]{2,1,0:T(8,128)(2,1)}), bf16[8,8,512]{2,1,0:T(8,128)(2,1)S(1)}, u32[]{:S(2)}, u32[]{:S(2)}) async-start(bf16[8,8,512]{2,1,0:T(8,128)(2,1)} %bitcast.96), calls=%async_computation.1 | async-start | bytes 131072 | tf_op jit(solution)/shard_map/all_to_all | solution.py:122
  8.1 6.2 %all-to-all-done.1 = bf16[8,8,512]{2,1,0:T(8,128)(2,1)S(1)} async-done(((bf16[8,8,512]{2,1,0:T(8,128)(2,1)}), bf16[8,8,512]{2,1,0:T(8,128)(2,1)S(1)}, u32[]{:S(2)}, u32[]{:S(2)}) %all-to-all-start.1) | async-done | bytes 65568 | tf_op jit(solution)/shard_map/all_to_all | solution.py:122
  14.3 3.4 %all-to-all-start.2 = ((bf16[8,8,512]{2,1,0:T(8,128)(2,1)}), bf16[8,8,512]{2,1,0:T(8,128)(2,1)S(1)}, u32[]{:S(2)}, u32[]{:S(2)}) async-start(bf16[8,8,512]{2,1,0:T(8,128)(2,1)} %bitcast.8), calls=%async_computation.2 | async-start | bytes 131072 | tf_op jit(solution)/shard_map/all_to_all | solution.py:123
  17.8 6.8 %all-to-all-done.2 = bf16[8,8,512]{2,1,0:T(8,128)(2,1)S(1)} async-done(((bf16[8,8,512]{2,1,0:T(8,128)(2,1)}), bf16[8,8,512]{2,1,0:T(8,128)(2,1)S(1)}, u32[]{:S(2)}, u32[]{:S(2)}) %all-to-all-start.2) | async-done | bytes 65568 | tf_op jit(solution)/shard_map/all_to_all | solution.py:123
  24.5 3.4 %all-to-all-start = ((bf16[8,8,512]{2,1,0:T(8,128)(2,1)}), bf16[8,8,512]{2,1,0:T(8,128)(2,1)S(1)}, u32[]{:S(2)}, u32[]{:S(2)}) async-start(bf16[8,8,512]{2,1,0:T(8,128)(2,1)} %bitcast.4), calls=%async_computation | async-start | bytes 131072 | tf_op jit(solution)/shard_map/all_to_all | solution.py:114
  28.0 6.7 %all-to-all-done = bf16[8,8,512]{2,1,0:T(8,128)(2,1)S(1)} async-done(((bf16[8,8,512]{2,1,0:T(8,128)(2,1)}), bf16[8,8,512]{2,1,0:T(8,128)(2,1)S(1)}, u32[]{:S(2)}, u32[]{:S(2)}) %all-to-all-start) | async-done | bytes 65568 | tf_op jit(solution)/shard_map/all_to_all | solution.py:114
  34.7 0.2 fusion.48
  35.0 0.2 fusion.47
  35.2 0.1 fusion.7
  35.4 0.3 fusion.3
  35.6 0.3 fusion
  36.1 0.1 div.60
  36.3 0.1 divide_convert_fusion
  36.4 0.2 constant_dynamic-slice_fusion
  36.6 0.5 collective-permute-start.1
  37.1 0.9 %collective-permute-start.2 = (bf16[1,8,512]{2,1,0:T(8,128)(2,1)S(1)}, bf16[1,8,512]{2,1,0:T(8,128)(2,1)S(1)}, u32[]{:S(2)}, u32[]{:S(2)}) collective-permute-start(bf16[1,8,512]{2,1,0:T(8,128)(2,1)S(1)} %bitcast.108), channel_id=1, source_target_pairs={{0,4},{2,6},{4,0},{6,2},{8,12},{10,14},{12,8},{14,10},{1,5},{3,7},... | collective-permute-start | bytes 24584 | tf_op jit(solution)/shard_map/ppermute | solution.py:29
  38.0 2.3 %collective-permute-start.3 = (bf16[1,8,512]{2,1,0:T(8,128)(2,1)S(1)}, bf16[1,8,512]{2,1,0:T(8,128)(2,1)S(1)}, u32[]{:S(2)}, u32[]{:S(2)}) collective-permute-start(bf16[1,8,512]{2,1,0:T(8,128)(2,1)S(1)} %bitcast.103), channel_id=1, source_target_pairs={{0,6},{2,4},{4,2},{6,0},{8,14},{10,12},{12,10},{14,8},{1,7},{3,5},... | collective-permute-start | bytes 24584 | tf_op jit(solution)/shard_map/ppermute | solution.py:29
  40.2 0.5 collective-permute-start.4
  40.7 2.3 %collective-permute-start.5 = (bf16[1,8,512]{2,1,0:T(8,128)(2,1)S(1)}, bf16[1,8,512]{2,1,0:T(8,128)(2,1)S(1)}, u32[]{:S(2)}, u32[]{:S(2)}) collective-permute-start(bf16[1,8,512]{2,1,0:T(8,128)(2,1)S(1)} %bitcast.99), channel_id=1, source_target_pairs={{0,10},{2,8},{4,14},{6,12},{8,2},{10,0},{12,6},{14,4},{1,11},{3,9}... | collective-permute-start | bytes 24584 | tf_op jit(solution)/shard_map/ppermute | solution.py:29
  43.0 1.0 %collective-permute-start.6 = (bf16[1,8,512]{2,1,0:T(8,128)(2,1)S(1)}, bf16[1,8,512]{2,1,0:T(8,128)(2,1)S(1)}, u32[]{:S(2)}, u32[]{:S(2)}) collective-permute-start(bf16[1,8,512]{2,1,0:T(8,128)(2,1)S(1)} %bitcast.98), channel_id=1, source_target_pairs={{0,12},{2,14},{4,8},{6,10},{8,4},{10,6},{12,0},{14,2},{1,13},{3,15... | collective-permute-start | bytes 24584 | tf_op jit(solution)/shard_map/ppermute | solution.py:29
  44.1 4.0 %collective-permute-start.7 = (bf16[1,8,512]{2,1,0:T(8,128)(2,1)S(1)}, bf16[1,8,512]{2,1,0:T(8,128)(2,1)S(1)}, u32[]{:S(2)}, u32[]{:S(2)}) collective-permute-start(bf16[1,8,512]{2,1,0:T(8,128)(2,1)S(1)} %bitcast.97), channel_id=1, source_target_pairs={{0,14},{2,12},{4,10},{6,8},{8,6},{10,4},{12,2},{14,0},{1,15},{3,13... | collective-permute-start | bytes 24584 | tf_op jit(solution)/shard_map/ppermute | solution.py:29
  48.2 0.3 collective-permute-done.6
  48.6 1.9 %collective-permute-done.7 = bf16[1,8,512]{2,1,0:T(8,128)(2,1)S(1)} collective-permute-done((bf16[1,8,512]{2,1,0:T(8,128)(2,1)S(1)}, bf16[1,8,512]{2,1,0:T(8,128)(2,1)S(1)}, u32[]{:S(2)}, u32[]{:S(2)}) %collective-permute-start.7) | collective-permute-done | bytes 8224 | tf_op jit(solution)/shard_map/ppermute | solution.py:29
  50.5 1.2 %gather_fusion = bf16[8,8,512]{2,1,0:T(8,128)(2,1)} fusion(bf16[8,8,512]{2,1,0:T(8,128)(2,1)S(1)} %bitcast.95, s32[1024]{0:T(1024)S(1)} %pad_clamp_fusion), kind=kCustom, calls=%fused_computation | custom fusion | bytes 131104 | tf_op jit(solution)/shard_map/gather | solution.py:30
  (50 shorter events, 1.3 us)
Async XLA Ops:
  0.0 7.9 %copy-start = (s32[32,1,1]{0,2,1:T(1,128)S(1)}, s32[32,1,1]{0,2,1:T(1,128)}, u32[]{:S(2)}) copy-start(s32[32,1,1]{0,2,1:T(1,128)} %param.11) | copy-start | bytes 388
  0.0 14.3 %all-to-all-start.1 = ((bf16[8,8,512]{2,1,0:T(8,128)(2,1)}), bf16[8,8,512]{2,1,0:T(8,128)(2,1)S(1)}, u32[]{:S(2)}, u32[]{:S(2)}) async-start(bf16[8,8,512]{2,1,0:T(8,128)(2,1)} %bitcast.96), calls=%async_computation.1 | async-start | bytes 131072 | tf_op jit(solution)/shard_map/all_to_all | solution.py:122
  14.3 10.2 %all-to-all-start.2 = ((bf16[8,8,512]{2,1,0:T(8,128)(2,1)}), bf16[8,8,512]{2,1,0:T(8,128)(2,1)S(1)}, u32[]{:S(2)}, u32[]{:S(2)}) async-start(bf16[8,8,512]{2,1,0:T(8,128)(2,1)} %bitcast.8), calls=%async_computation.2 | async-start | bytes 131072 | tf_op jit(solution)/shard_map/all_to_all | solution.py:123
  24.5 10.2 %all-to-all-start = ((bf16[8,8,512]{2,1,0:T(8,128)(2,1)}), bf16[8,8,512]{2,1,0:T(8,128)(2,1)S(1)}, u32[]{:S(2)}, u32[]{:S(2)}) async-start(bf16[8,8,512]{2,1,0:T(8,128)(2,1)} %bitcast.4), calls=%async_computation | async-start | bytes 131072 | tf_op jit(solution)/shard_map/all_to_all | solution.py:114
  27.9 7.0 %collective-permute-start = (bf16[2,8,8,512]{3,2,1,0:T(8,128)(2,1)S(1)}, bf16[2,8,8,512]{3,2,1,0:T(8,128)(2,1)S(1)}, u32[]{:S(2)}, u32[]{:S(2)}) collective-permute-start(bf16[2,8,8,512]{3,2,1,0:T(8,128)(2,1)S(1)} %pad_maximum_fusion), channel_id=1, source_target_pairs={{0,1},{1,0},{2,3},{3,2},{4,5},{5,4},{6,7},{7,6},{8,9},{9,8},{10,11... | collective-permute-start | bytes 393224 | tf_op jit(solution)/shard_map/ppermute | solution.py:36
  36.6 6.4 %collective-permute-start.1 = (bf16[1,8,512]{2,1,0:T(8,128)(2,1)S(1)}, bf16[1,8,512]{2,1,0:T(8,128)(2,1)S(1)}, u32[]{:S(2)}, u32[]{:S(2)}) collective-permute-start(bf16[1,8,512]{2,1,0:T(8,128)(2,1)S(1)} %bitcast.110), channel_id=1, source_target_pairs={{0,2},{2,0},{4,6},{6,4},{8,10},{10,8},{12,14},{14,12},{1,3},{3,1},... | collective-permute-start | bytes 24584 | tf_op jit(solution)/shard_map/ppermute | solution.py:29
  37.1 7.0 %collective-permute-start.2 = (bf16[1,8,512]{2,1,0:T(8,128)(2,1)S(1)}, bf16[1,8,512]{2,1,0:T(8,128)(2,1)S(1)}, u32[]{:S(2)}, u32[]{:S(2)}) collective-permute-start(bf16[1,8,512]{2,1,0:T(8,128)(2,1)S(1)} %bitcast.108), channel_id=1, source_target_pairs={{0,4},{2,6},{4,0},{6,2},{8,12},{10,14},{12,8},{14,10},{1,5},{3,7},... | collective-permute-start | bytes 24584 | tf_op jit(solution)/shard_map/ppermute | solution.py:29
  38.0 10.1 %collective-permute-start.3 = (bf16[1,8,512]{2,1,0:T(8,128)(2,1)S(1)}, bf16[1,8,512]{2,1,0:T(8,128)(2,1)S(1)}, u32[]{:S(2)}, u32[]{:S(2)}) collective-permute-start(bf16[1,8,512]{2,1,0:T(8,128)(2,1)S(1)} %bitcast.103), channel_id=1, source_target_pairs={{0,6},{2,4},{4,2},{6,0},{8,14},{10,12},{12,10},{14,8},{1,7},{3,5},... | collective-permute-start | bytes 24584 | tf_op jit(solution)/shard_map/ppermute | solution.py:29
  40.2 7.9 %collective-permute-start.4 = (bf16[1,8,512]{2,1,0:T(8,128)(2,1)S(1)}, bf16[1,8,512]{2,1,0:T(8,128)(2,1)S(1)}, u32[]{:S(2)}, u32[]{:S(2)}) collective-permute-start(bf16[1,8,512]{2,1,0:T(8,128)(2,1)S(1)} %bitcast.101), channel_id=1, source_target_pairs={{0,8},{2,10},{4,12},{6,14},{8,0},{10,2},{12,4},{14,6},{1,9},{3,11}... | collective-permute-start | bytes 24584 | tf_op jit(solution)/shard_map/ppermute | solution.py:29
  40.7 7.4 %collective-permute-start.5 = (bf16[1,8,512]{2,1,0:T(8,128)(2,1)S(1)}, bf16[1,8,512]{2,1,0:T(8,128)(2,1)S(1)}, u32[]{:S(2)}, u32[]{:S(2)}) collective-permute-start(bf16[1,8,512]{2,1,0:T(8,128)(2,1)S(1)} %bitcast.99), channel_id=1, source_target_pairs={{0,10},{2,8},{4,14},{6,12},{8,2},{10,0},{12,6},{14,4},{1,11},{3,9}... | collective-permute-start | bytes 24584 | tf_op jit(solution)/shard_map/ppermute | solution.py:29
  43.0 5.5 %collective-permute-start.6 = (bf16[1,8,512]{2,1,0:T(8,128)(2,1)S(1)}, bf16[1,8,512]{2,1,0:T(8,128)(2,1)S(1)}, u32[]{:S(2)}, u32[]{:S(2)}) collective-permute-start(bf16[1,8,512]{2,1,0:T(8,128)(2,1)S(1)} %bitcast.98), channel_id=1, source_target_pairs={{0,12},{2,14},{4,8},{6,10},{8,4},{10,6},{12,0},{14,2},{1,13},{3,15... | collective-permute-start | bytes 24584 | tf_op jit(solution)/shard_map/ppermute | solution.py:29
  44.1 6.4 %collective-permute-start.7 = (bf16[1,8,512]{2,1,0:T(8,128)(2,1)S(1)}, bf16[1,8,512]{2,1,0:T(8,128)(2,1)S(1)}, u32[]{:S(2)}, u32[]{:S(2)}) collective-permute-start(bf16[1,8,512]{2,1,0:T(8,128)(2,1)S(1)} %bitcast.97), channel_id=1, source_target_pairs={{0,14},{2,12},{4,10},{6,8},{8,6},{10,4},{12,2},{14,0},{1,15},{3,13... | collective-permute-start | bytes 24584 | tf_op jit(solution)/shard_map/ppermute | solution.py:29
